TPU v7x, 32 devices: a whole 2x2x4 slice. The times are simulated.
32 devices in a mesh: row: 8 (over z, x), col: 4 (over y, core).
Axes of the slice: x: 2, y: 2, z: 4, core: 2. Of those that a mesh axis runs over, the one named last changes fastest.
Arguments:
- hamiltonian: bfloat16 [2, 2048, 2048], P(None, 'row', 'col'), may hold values from -0.25 to 0.25
- basis_metric: bfloat16 [2048, 2048], P('row', 'col'), may hold values from -0.25 to 0.25
- density: bfloat16 [2, 2048, 2048], P(None, 'row', 'col'), may hold values from -6 to 6
- hamiltonian_keep: int32 [16, 16], P('row', 'col'), may hold values from 0 to 1, as said below
- metric_keep: int32 [16, 16], P('row', 'col'), may hold values from 0 to 1, as said below
- density_keep: int32 [16, 16], P('row', 'col'), may hold values from 0 to 1, as said below
- gradient_keep: int32 [16, 16], P('row', 'col'), may hold values 0 or 1
Outputs:
- gradient: float32 [2, 2048, 2048], P(None, 'row', 'col')
Inputs may be any that keep to these rules, and one draw needn't show every extreme that they name: `hamiltonian_keep`: each block row has at most 4 blocks in the pattern, and some rows have exactly 4. `metric_keep`: each block row has at most 4 blocks in the pattern, and some rows have exactly 4. `density_keep`: each block row keeps at most 7 blocks, and some rows keep exactly 7.
All inputs are finite; a program needn't handle non-finite values. No bound on the sum of `gradient_keep` on one device may be relied on, other than what follows from the above.
Results may differ from a plain program's by a relative error of at most 0.0029.
Values may be sent and summed in bfloat16 or wider, within the bound.
No kernel may reach another device: no remote copies, remote signals or barrier semaphores. Data moves between devices by JAX's collectives and lax.ppermute only.
A program may use at most 64 MiB of HBM per device.

v0:
```python
import jax
import jax.numpy as jnp
from jax import lax
from jax.sharding import PartitionSpec as P

BLOCK = 128


def widen(keep):
    return jnp.repeat(jnp.repeat(keep, BLOCK, axis=0), BLOCK, axis=1) > 0


def first_terms(rows_part, cols_part):
    hterm = jnp.einsum("srl,slc->src", rows_part[:2], cols_part, preferred_element_type=jnp.float32)
    sterm = jnp.einsum("rl,slc->src", rows_part[2], cols_part, preferred_element_type=jnp.float32)
    return jnp.concatenate([hterm, sterm], axis=0)


def second_terms(rows_part, cols_part):
    left = jnp.einsum(
        "srl,lc->src", rows_part[:2], cols_part[2], preferred_element_type=jnp.float32
    )
    right = jnp.einsum(
        "srl,slc->src", rows_part[2:], cols_part[:2], preferred_element_type=jnp.float32
    )
    return left - right


def body(
    hamiltonian, basis_metric, density, hamiltonian_keep, metric_keep, density_keep, gradient_keep
):
    kohn_sham = jnp.where(widen(hamiltonian_keep)[None], hamiltonian, jnp.zeros_like(hamiltonian))
    smat = jnp.where(widen(metric_keep), basis_metric, jnp.zeros_like(basis_metric))
    filtered = jnp.where(widen(density_keep)[None], density, jnp.zeros_like(density))
    operators = jnp.concatenate([kohn_sham, smat[None]], axis=0)
    density_cols = lax.all_gather(filtered, "row", axis=1, tiled=True)
    cols_part = density_cols
    products = first_terms(lax.all_gather(operators, "col", axis=2, tiled=True), cols_part)
    products = products.astype(jnp.bfloat16)
    operator_cols = lax.all_gather(operators, "row", axis=1, tiled=True)
    cols_part = operator_cols
    commut = second_terms(lax.all_gather(products, "col", axis=2, tiled=True), cols_part)
    grad_mask = widen(gradient_keep)[None]
    return jnp.where(grad_mask, commut, jnp.zeros_like(commut))


def solution(mesh):
    in_specs = (
        P(None, "row", "col"),
        P("row", "col"),
        P(None, "row", "col"),
        P("row", "col"),
        P("row", "col"),
        P("row", "col"),
        P("row", "col"),
    )
    out_specs = P(None, "row", "col")
    return jax.shard_map(body, mesh=mesh, in_specs=in_specs, out_specs=out_specs, check_vma=False)
```

profile of v0, /device:TPU:0, one launch (start us, length us, event | category | flops | bytes accessed | tf_op | source)
XLA Modules:
  0.0 267.1 jit_solution(11964594302407016854)
XLA Ops:
  6.5 0.0 copy-start.4
  6.5 0.0 copy-start
  6.5 0.0 all-gather.5.cloned.1.call-start
  6.5 0.7 broadcast_compare_fusion.2
  7.3 0.3 broadcast_in_dim.61
  7.6 0.1 copy.23
  7.7 0.7 broadcast_compare_fusion.1
  8.4 1.1 broadcast_select_fusion.1
  9.5 0.3 broadcast_in_dim.64
  9.9 1.0 fusion.6
  10.9 1.0 pad_maximum_fusion.1
  11.9 0.0 all-gather.5.cloned.1.call-update
  11.9 0.0 all-gather.7.cloned.1.call-start
  11.9 0.0 copy-done.4
  12.0 0.3 broadcast_in_dim.68
  12.3 0.1 copy.22
  12.4 0.0 copy-done
  12.4 0.9 broadcast_select_fusion
  13.2 0.0 all-gather.7.cloned.1.call-update
  13.3 0.0 all-gather.11.cloned.1.call-start
  13.3 0.7 all-gather.11.cloned.1.call-update
  14.0 0.0 all-gather.9.cloned.1.call-start
  14.1 29.2 %all-gather.5.cloned.1.call-done = bf16[3,256,2048]{2,1,0:T(8,128)(2,1)} async-done(((bf16[3,256,512]{2,1,0:T(8,128)(2,1)}), bf16[3,256,2048]{2,1,0:T(8,128)(2,1)}) %all-gather.5.cloned.1.call-update) | async-done | bytes 3145744 | tf_op jit(solution)/shard_map/all_gather | solution.py:38
  43.3 0.0 copy-start.3
  43.3 75.6 %all-gather.7.cloned.1.call-done = bf16[2,2048,512]{2,1,0:T(8,128)(2,1)} async-done(((bf16[2,256,512]{2,1,0:T(8,128)(2,1)}), bf16[2,2048,512]{2,1,0:T(8,128)(2,1)}) %all-gather.7.cloned.1.call-update) | async-done | bytes 4194320 | tf_op jit(solution)/shard_map/all_gather | solution.py:36
  118.9 0.0 copy-start.1
  118.9 3.9 %fusion.5 = bf16[2,256,512]{2,1,0:T(8,128)(2,1)S(1)} fusion(bf16[2,2048,512]{2,1,0:T(8,128)(2,1)} %all-gather.7.cloned.1.call-done, bf16[3,256,2048]{2,1,0:T(8,128)(2,1)} %all-gather.5.cloned.1.call-done), kind=kOutput, calls=%fused_computation.8 | convolution fusion | flops 1074003968 | bytes 5767168 | tf_op jit(solution)/shard_map/rl,slc->src/dot_general | solution.py:15
  122.8 0.0 copy-done.3
  122.8 0.0 copy-done.1
  122.8 0.0 copy-start.5
  122.8 1.3 convolution_convert_fusion
  124.1 1.1 pad_maximum_fusion
  125.2 0.0 all-gather.9.cloned.1.call-update
  125.2 0.0 copy-done.5
  125.2 0.3 broadcast_in_dim.58
  125.6 0.1 copy.24
  125.6 92.7 %all-gather.11.cloned.1.call-done = bf16[3,2048,512]{2,1,0:T(8,128)(2,1)} async-done(((bf16[3,256,512]{2,1,0:T(8,128)(2,1)}), bf16[3,2048,512]{2,1,0:T(8,128)(2,1)}) %all-gather.11.cloned.1.call-update) | async-done | bytes 6291472 | tf_op jit(solution)/shard_map/all_gather | solution.py:40
  218.4 34.1 %all-gather.9.cloned.1.call-done = bf16[4,256,2048]{2,1,0:T(8,128)(2,1)} async-done(((bf16[4,256,512]{2,1,0:T(8,128)(2,1)}), bf16[4,256,2048]{2,1,0:T(8,128)(2,1)}) %all-gather.9.cloned.1.call-update) | async-done | bytes 4194320 | tf_op jit(solution)/shard_map/all_gather | solution.py:42
  252.5 0.0 copy-start.2
  252.5 4.2 %fusion = f32[2,256,512]{2,1,0:T(8,128)S(1)} fusion(bf16[4,256,2048]{2,1,0:T(8,128)(2,1)} %all-gather.9.cloned.1.call-done, bf16[3,2048,512]{2,1,0:T(8,128)(2,1)} %all-gather.11.cloned.1.call-done), kind=kOutput, calls=%fused_computation | convolution fusion | flops 1073741824 | bytes 9437184 | tf_op jit(solution)/shard_map/srl,slc->src/dot_general | solution.py:23
  256.7 0.0 copy-done.2
  256.7 3.8 %fusion.4 = f32[2,256,512]{2,1,0:T(8,128)} fusion(f32[2,256,512]{2,1,0:T(8,128)S(1)} %fusion, bf16[4,256,2048]{2,1,0:T(8,128)(2,1)S(1)} %copy-done.2, bf16[3,2048,512]{2,1,0:T(8,128)(2,1)} %all-gather.11.cloned.1.call-done, pred[256,512]{1,0:T(8,128)(4,1)S(1)} %bitcast.52), kind=kOutput, calls=%fused_computation.5 | convolution fusion | flops 1074266112 | bytes 8519680 | tf_op jit(solution)/shard_map/srl,lc->src/dot_general | solution.py:20
  (6 shorter events, 0.1 us)
Async XLA Ops:
  6.5 5.4 %copy-start.4 = (s32[2,4]{1,0:T(2,128)S(1)}, s32[2,4]{1,0:T(2,128)}, u32[]{:S(2)}) copy-start(s32[2,4]{1,0:T(2,128)} %param.12) | copy-start | bytes 100
  6.5 5.9 %copy-start = (bf16[2,256,512]{2,1,0:T(8,128)(2,1)S(1)}, bf16[2,256,512]{2,1,0:T(8,128)(2,1)}, u32[]{:S(2)}) copy-start(bf16[2,256,512]{2,1,0:T(8,128)(2,1)} %param.9) | copy-start | bytes 1572868
  6.5 36.7 %all-gather.5.cloned.1.call-start = ((), (), s32[]{:S(2)}) async-start(), calls=%async_computation | async-start | bytes 3932160 | tf_op jit(solution)/shard_map/all_gather | solution.py:38
  11.9 107.0 %all-gather.7.cloned.1.call-start = ((), (), s32[]{:S(2)}) async-start(), calls=%async_computation.1 | async-start | bytes 4718592 | tf_op jit(solution)/shard_map/all_gather | solution.py:36
  13.3 205.1 %all-gather.11.cloned.1.call-start = ((), (), s32[]{:S(2)}) async-start(), calls=%async_computation.3 | async-start | bytes 7077888 | tf_op jit(solution)/shard_map/all_gather | solution.py:40
  14.0 238.5 %all-gather.9.cloned.1.call-start = ((), (), s32[]{:S(2)}) async-start(), calls=%async_computation.2 | async-start | bytes 5242880 | tf_op jit(solution)/shard_map/all_gather | solution.py:42
  43.3 79.5 %copy-start.3 = (bf16[3,256,2048]{2,1,0:T(8,128)(2,1)S(1)}, bf16[3,256,2048]{2,1,0:T(8,128)(2,1)}, u32[]{:S(2)}) copy-start(bf16[3,256,2048]{2,1,0:T(8,128)(2,1)} %all-gather.5.cloned.1.call-done) | copy-start | bytes 9437188
  118.9 3.9 %copy-start.1 = (bf16[2,2048,512]{2,1,0:T(8,128)(2,1)S(1)}, bf16[2,2048,512]{2,1,0:T(8,128)(2,1)}, u32[]{:S(2)}) copy-start(bf16[2,2048,512]{2,1,0:T(8,128)(2,1)} %all-gather.7.cloned.1.call-done) | copy-start | bytes 12582916
  122.8 2.4 copy-start.5
  252.5 4.2 %copy-start.2 = (bf16[4,256,2048]{2,1,0:T(8,128)(2,1)S(1)}, bf16[4,256,2048]{2,1,0:T(8,128)(2,1)}, u32[]{:S(2)}) copy-start(bf16[4,256,2048]{2,1,0:T(8,128)(2,1)} %all-gather.9.cloned.1.call-done) | copy-start | bytes 12582916
Sparse Core Ops, SparseCore 0:
  12.0 31.2 all-gather.4
  45.5 73.3 all-gather.6
  121.0 97.2 all-gather.10
  219.8 32.6 all-gather.8
where the time goes:
time: 267 us
  waiting for transfers between devices  232 us (87%)
  matrix products  13.3 us (5%)
  between operations  13.3 us (5%)
  other arithmetic  6.44 us (2%)
    all_gather x1, waiting for transfers between devices, body(): operator_cols = lax.all_gather(operators, 'row', axis=1, tiled=True)  92.7 us
    all_gather x1, waiting for transfers between devices, body(): density_cols = lax.all_gather(filtered, 'row', axis=1, tiled=True)  75.6 us
    all_gather x1, waiting for transfers between devices, body(): lax.all_gather(products, 'col', axis=2, tiled=True)  34.1 us
    all_gather x1, waiting for transfers between devices, body(): lax.all_gather(operators, 'col', axis=2, tiled=True)  29.2 us
  transfers between devices with their start and end apart: 4, of which 4 were waited for; matrix products, arithmetic and copies ran while one was open for 3% of the time, Pallas kernels for 0%

commit v1 on v0

--- a/solution.py
+++ b/solution.py
@@ -4,6 +4,22 @@
 from jax.sharding import PartitionSpec as P
 
 BLOCK = 128
+
+
+def answer_field(mine):
+    n_peers_all = lax.axis_size("col")
+    table = [(src_i, (src_i + 1) % n_peers_all) for src_i in range(n_peers_all)]
+    stack_in = [(src_i, (src_i - 1) % n_peers_all) for src_i in range(n_peers_all)]
+    now, block_next = ([mine], [mine])
+    for _ in range(n_peers_all // 2):
+        now.append(lax.ppermute(now[-1], axis_name="col", perm=table))
+    for _ in range((n_peers_all - 1) // 2):
+        block_next.append(lax.ppermute(block_next[-1], axis_name="col", perm=stack_in))
+    field_out = jnp.concatenate([*now[::-1], *block_next[1:]], axis=2)
+    finding = jnp.roll(
+        field_out, shift=(lax.axis_index("col") - n_peers_all // 2) * mine.shape[2], axis=2
+    )
+    return finding
 
 
 def widen(keep):
@@ -35,7 +51,7 @@
     operators = jnp.concatenate([kohn_sham, smat[None]], axis=0)
     density_cols = lax.all_gather(filtered, "row", axis=1, tiled=True)
     cols_part = density_cols
-    products = first_terms(lax.all_gather(operators, "col", axis=2, tiled=True), cols_part)
+    products = first_terms(answer_field(operators), cols_part)
     products = products.astype(jnp.bfloat16)
     operator_cols = lax.all_gather(operators, "row", axis=1, tiled=True)
     cols_part = operator_cols

time: 267 us -> 235 us (0.88)
  waiting for transfers between devices: 232 us -> 186 us
  local copies, waits for them, and re-layouts: 1.63 us -> 7.6 us
  other arithmetic: 6.44 us -> 10.1 us
    all_gather x1, waiting for transfers between devices: 75.6 us -> 33.6 us  [body(): density_cols = lax.all_gather(filtered, 'row', axis=1, tiled=True)]
    all_gather x1 -> x0, waiting for transfers between devices: 29.2 us -> none  [body(): lax.all_gather(operators, 'col', axis=2, tiled=True)]
    ppermute x0 -> x3, waiting for transfers between devices: none -> 27.1 us  [the longest x2 27.1 us: answer_field(): now.append(lax.ppermute(now[-1], axis_name='col', perm=table))]
    unnamed x15 -> x14, local copies, waits for them, and re-layouts: 0.23 us -> 5.24 us
  transfers between devices with their start and end apart: 4 -> 6, of which waited for: 4 -> 5; matrix products, arithmetic and copies ran while one was open for 3% -> 9% of each run, Pallas kernels for 0% -> 0%
where the time goes in v1:
time: 235 us; the launch traced here: 234 us
  waiting for transfers between devices  186 us (79%)
  matrix products  14.9 us (6%)
  between operations  13.2 us (6%)
  other arithmetic  10.1 us (4%)
  local copies, waits for them, and re-layouts  7.6 us (3%)
    all_gather x1, waiting for transfers between devices, body(): operator_cols = lax.all_gather(operators, 'row', axis=1, tiled=True)  91.1 us
    all_gather x1, waiting for transfers between devices, body(): lax.all_gather(products, 'col', axis=2, tiled=True)  34.3 us
    all_gather x1, waiting for transfers between devices, body(): density_cols = lax.all_gather(filtered, 'row', axis=1, tiled=True)  33.6 us
    ppermute x2, waiting for transfers between devices, answer_field(): now.append(lax.ppermute(now[-1], axis_name='col', perm=table))  27.1 us
    unnamed x14, local copies, waits for them, and re-layouts  5.24 us
  transfers between devices with their start and end apart: 6, of which 5 were waited for; matrix products, arithmetic and copies ran while one was open for 9% of the time, Pallas kernels for 0%

profile of v1, /device:TPU:0, one launch (start us, length us, event | category | flops | bytes accessed | tf_op | source)
XLA Modules:
  0.0 234.2 jit_solution(5810524558689671142)
XLA Ops:
  6.5 0.0 all-gather.4.cloned.1.call-start
  6.5 0.7 broadcast_compare_fusion
  7.2 0.3 broadcast_in_dim.68
  7.6 0.1 copy.22
  7.7 1.9 broadcast_select_fusion
  9.5 0.0 all-gather.4.cloned.1.call-update
  9.6 0.0 all-gather.8.cloned.1.call-start
  9.6 0.7 broadcast_compare_fusion.2
  10.3 0.3 broadcast_in_dim.61
  10.7 0.1 copy.23
  10.7 0.7 broadcast_compare_fusion.1
  11.4 0.3 broadcast_in_dim.64
  11.8 1.0 fusion.11
  12.8 1.1 broadcast_select_fusion.1
  13.9 1.0 pad_maximum_fusion.1
  14.9 0.0 all-gather.8.cloned.1.call-update
  14.9 0.0 all-gather.6.cloned.1.call-start
  15.0 0.5 collective-permute-start
  15.5 11.8 %collective-permute-done = bf16[3,256,512]{2,1,0:T(8,128)(2,1)S(1)} collective-permute-done((bf16[3,256,512]{2,1,0:T(8,128)(2,1)}, bf16[3,256,512]{2,1,0:T(8,128)(2,1)S(1)}, u32[]{:S(2)}, u32[]{:S(2)}) %collective-permute-start) | collective-permute-done | bytes 786464 | tf_op jit(solution)/shard_map/ppermute | solution.py:15
  27.3 0.0 collective-permute-start.1
  27.4 1.7 collective-permute-start.2
  29.1 15.2 %collective-permute-done.1 = bf16[3,256,512]{2,1,0:T(8,128)(2,1)S(1)} collective-permute-done((bf16[3,256,512]{2,1,0:T(8,128)(2,1)S(1)}, bf16[3,256,512]{2,1,0:T(8,128)(2,1)S(1)}, u32[]{:S(2)}, u32[]{:S(2)}) %collective-permute-start.1) | collective-permute-done | bytes 786464 | tf_op jit(solution)/shard_map/ppermute | solution.py:15
  44.3 1.0 constant_dynamic-update-slice_fusion.7
  45.3 1.0 constant_dynamic-update-slice_fusion.6
  46.3 1.0 constant_dynamic-update-slice_fusion.5
  47.3 0.0 collective-permute-done.2
  47.3 1.0 constant_dynamic-update-slice_fusion.4
  48.3 1.0 constant_dynamic-update-slice_fusion.3
  49.3 1.0 constant_dynamic-update-slice_fusion.2
  50.3 1.0 constant_dynamic-update-slice_fusion.1
  51.3 0.9 constant_dynamic-update-slice_fusion
  52.2 33.6 %all-gather.4.cloned.1.call-done = bf16[2,2048,512]{2,1,0:T(8,128)(2,1)} async-done(((bf16[2,256,512]{2,1,0:T(8,128)(2,1)}), bf16[2,2048,512]{2,1,0:T(8,128)(2,1)}) %all-gather.4.cloned.1.call-update) | async-done | bytes 4194320 | tf_op jit(solution)/shard_map/all_gather | solution.py:52
  85.8 0.0 copy-start
  85.8 3.9 %fusion.10 = bf16[2,256,512]{2,1,0:T(8,128)(2,1)S(1)} fusion(bf16[2,2048,512]{2,1,0:T(8,128)(2,1)} %all-gather.4.cloned.1.call-done, bf16[3,256,4096]{2,1,0:T(8,128)(2,1)} %constant_dynamic-update-slice_fusion, s32[]{:T(128)S(6)} %add.13, s32[]{:T(128)S(6)} %select_n.31), kind=kOutput, calls=%fused_computation.10 | convolution fusion | flops 1074003968 | bytes 5767176 | tf_op jit(solution)/shard_map/rl,slc->src/dot_general | solution.py:31
  89.7 0.0 copy-done
  89.7 0.0 copy-start.2
  89.7 2.9 %fusion.7 = bf16[2,256,512]{2,1,0:T(8,128)(2,1)S(1)} fusion(bf16[2,2048,512]{2,1,0:T(8,128)(2,1)S(1)} %copy-done, bf16[3,256,4096]{2,1,0:T(8,128)(2,1)} %constant_dynamic-update-slice_fusion, s32[]{:T(128)S(6)} %select_n.31), kind=kOutput, calls=%fused_computation.8 | convolution fusion | flops 1074003968 | bytes 7864324 | tf_op jit(solution)/shard_map/srl,slc->src/dot_general | solution.py:30
  92.6 1.1 pad_maximum_fusion
  93.7 0.0 all-gather.6.cloned.1.call-update
  93.7 0.0 copy-done.2
  93.8 0.3 broadcast_in_dim.58
  94.1 0.1 copy.24
  94.2 91.1 %all-gather.8.cloned.1.call-done = bf16[3,2048,512]{2,1,0:T(8,128)(2,1)} async-done(((bf16[3,256,512]{2,1,0:T(8,128)(2,1)}), bf16[3,2048,512]{2,1,0:T(8,128)(2,1)}) %all-gather.8.cloned.1.call-update) | async-done | bytes 6291472 | tf_op jit(solution)/shard_map/all_gather | solution.py:56
  185.3 34.3 %all-gather.6.cloned.1.call-done = bf16[4,256,2048]{2,1,0:T(8,128)(2,1)} async-done(((bf16[4,256,512]{2,1,0:T(8,128)(2,1)}), bf16[4,256,2048]{2,1,0:T(8,128)(2,1)}) %all-gather.6.cloned.1.call-update) | async-done | bytes 4194320 | tf_op jit(solution)/shard_map/all_gather | solution.py:58
  219.6 0.0 copy-start.1
  219.6 4.2 %fusion = f32[2,256,512]{2,1,0:T(8,128)S(1)} fusion(bf16[4,256,2048]{2,1,0:T(8,128)(2,1)} %all-gather.6.cloned.1.call-done, bf16[3,2048,512]{2,1,0:T(8,128)(2,1)} %all-gather.8.cloned.1.call-done), kind=kOutput, calls=%fused_computation | convolution fusion | flops 1073741824 | bytes 9437184 | tf_op jit(solution)/shard_map/srl,slc->src/dot_general | solution.py:39
  223.8 0.0 copy-done.1
  223.8 3.8 %fusion.6 = f32[2,256,512]{2,1,0:T(8,128)} fusion(f32[2,256,512]{2,1,0:T(8,128)S(1)} %fusion, bf16[4,256,2048]{2,1,0:T(8,128)(2,1)S(1)} %copy-done.1, bf16[3,2048,512]{2,1,0:T(8,128)(2,1)} %all-gather.8.cloned.1.call-done, pred[256,512]{1,0:T(8,128)(4,1)S(1)} %bitcast.51), kind=kOutput, calls=%fused_computation.7 | convolution fusion | flops 1074266112 | bytes 8519680 | tf_op jit(solution)/shard_map/srl,lc->src/dot_general | solution.py:36
  (5 shorter events, 0.1 us)
Async XLA Ops:
  6.5 79.3 %all-gather.4.cloned.1.call-start = ((), (), s32[]{:S(2)}) async-start(), calls=%async_computation | async-start | bytes 4718592 | tf_op jit(solution)/shard_map/all_gather | solution.py:52
  9.6 175.7 %all-gather.8.cloned.1.call-start = ((), (), s32[]{:S(2)}) async-start(), calls=%async_computation.2 | async-start | bytes 7077888 | tf_op jit(solution)/shard_map/all_gather | solution.py:56
  14.9 204.7 %all-gather.6.cloned.1.call-start = ((), (), s32[]{:S(2)}) async-start(), calls=%async_computation.1 | async-start | bytes 5242880 | tf_op jit(solution)/shard_map/all_gather | solution.py:58
  15.0 12.3 %collective-permute-start = (bf16[3,256,512]{2,1,0:T(8,128)(2,1)}, bf16[3,256,512]{2,1,0:T(8,128)(2,1)S(1)}, u32[]{:S(2)}, u32[]{:S(2)}) collective-permute-start(bf16[3,256,512]{2,1,0:T(8,128)(2,1)} %pad_maximum_fusion.1), channel_id=1, source_target_pairs={{0,1},{1,2},{2,3},{3,0},{4,5},{5,6},{6,7},{7,4},{8,9},{9,10},{10,1... | collective-permute-start | bytes 2359304 | tf_op jit(solution)/shard_map/ppermute | solution.py:15
  27.3 17.0 %collective-permute-start.1 = (bf16[3,256,512]{2,1,0:T(8,128)(2,1)S(1)}, bf16[3,256,512]{2,1,0:T(8,128)(2,1)S(1)}, u32[]{:S(2)}, u32[]{:S(2)}) collective-permute-start(bf16[3,256,512]{2,1,0:T(8,128)(2,1)S(1)} %collective-permute-done), channel_id=1, source_target_pairs={{0,1},{1,2},{2,3},{3,0},{4,5},{5,6},{6,7},{7,4},{8,9},{9,10},{10,1... | collective-permute-start | bytes 2359304 | tf_op jit(solution)/shard_map/ppermute | solution.py:15
  27.4 20.0 %collective-permute-start.2 = (bf16[3,256,512]{2,1,0:T(8,128)(2,1)}, bf16[3,256,512]{2,1,0:T(8,128)(2,1)S(1)}, u32[]{:S(2)}, u32[]{:S(2)}) collective-permute-start(bf16[3,256,512]{2,1,0:T(8,128)(2,1)} %pad_maximum_fusion.1), channel_id=1, source_target_pairs={{0,3},{1,0},{2,1},{3,2},{4,7},{5,4},{6,5},{7,6},{8,11},{9,8},{10,9... | collective-permute-start | bytes 2359304 | tf_op jit(solution)/shard_map/ppermute | solution.py:17
  85.8 3.9 %copy-start = (bf16[2,2048,512]{2,1,0:T(8,128)(2,1)S(1)}, bf16[2,2048,512]{2,1,0:T(8,128)(2,1)}, u32[]{:S(2)}) copy-start(bf16[2,2048,512]{2,1,0:T(8,128)(2,1)} %all-gather.4.cloned.1.call-done) | copy-start | bytes 12582916
  89.7 4.0 %copy-start.2 = (s32[2,4]{1,0:T(2,128)S(1)}, s32[2,4]{1,0:T(2,128)}, u32[]{:S(2)}) copy-start(s32[2,4]{1,0:T(2,128)} %param.13) | copy-start | bytes 100
  219.6 4.2 %copy-start.1 = (bf16[4,256,2048]{2,1,0:T(8,128)(2,1)S(1)}, bf16[4,256,2048]{2,1,0:T(8,128)(2,1)}, u32[]{:S(2)}) copy-start(bf16[4,256,2048]{2,1,0:T(8,128)(2,1)} %all-gather.6.cloned.1.call-done) | copy-start | bytes 12582916
Sparse Core Ops, SparseCore 0:
  9.7 76.0 all-gather.3
  88.0 97.2 all-gather.7
  186.9 32.6 all-gather.5
